TPU v7x, 32 devices: a whole 2x2x4 slice. The times are simulated.
32 devices in a mesh: groups: 2 (over y), blk: 4 (over z), dp: 2 (over x), sub: 2 (over core).
Axes of the slice: x: 2, y: 2, z: 4, core: 2. Of those that a mesh axis runs over, the one named last changes fastest.
Arguments:
- view_a: bfloat16 [2048, 256], P(('groups', 'blk', 'dp', 'sub')), parts along dimension 0, may hold values from -6 to 6
- view_b: bfloat16 [2048, 256], P(('groups', 'blk', 'dp', 'sub')), parts along dimension 0, may hold values from -6 to 6
- prototypes: bfloat16 [32768, 256], P('blk'), may hold values from -6 to 6
- tile_mask: int32 [16, 256], replicated, may hold values from 0 to 1, as said below
- tile_region: int32 [32], P('groups'), parts along dimension 0, may hold values from 0 to 15, as said below
Outputs:
- grad_view_b: float32 [2048, 256], P(('groups', 'blk', 'dp', 'sub')), parts along dimension 0
- grad_prototypes: float32 [65536, 256], P(('groups', 'blk', 'dp', 'sub')), parts along dimension 0
There are 2 independent parts, one for each index of `groups`. A program takes and returns all parts, laid end to end along the dimension named above; an argument that names none is the same for every part. Nothing has to cross between parts.
Inputs may be any that keep to these rules, and one draw needn't show every extreme that they name: `tile_mask`: every prototype tile is 1 for at least one region, and every region for at least 16 tiles. `tile_region`: every region is named by at least one hit tile.
All inputs are finite; a program needn't handle non-finite values.
Results may differ from a plain program's by a relative error of at most 0.00045.
The roundings to bfloat16 on the way count: a program that leaves them out, or rounds other values in their place, can miss the bound.
Values may be sent and summed in bfloat16 or wider, within the bound.
A program may use at most 64 MiB of HBM per device.

v0:
```python
import jax
import jax.numpy as jnp
from jax import lax
from jax.sharding import PartitionSpec as P

TILE = 128
ITERS = 3
SOFTMAX_TEMPER = 0.1
EPSILON = 0.05
PART = ("blk", "dp", "sub")


def unit_rows(matrix):
    values = matrix.astype(jnp.float32)
    return (values * lax.rsqrt(jnp.sum(values * values, axis=1, keepdims=True) + 1e-06)).astype(
        jnp.bfloat16
    )


def body(view_a, view_b, prototypes, tile_mask, tile_region):
    n_dp = lax.axis_size("dp")
    n_sub = lax.axis_size("sub")
    blk_pos = lax.axis_index("blk")
    inner_pos = lax.axis_index("dp") * n_sub + lax.axis_index("sub")
    hit_dev, width = view_a.shape
    cols = prototypes.shape[0] // (n_dp * n_sub)
    tiles = cols // TILE
    regions = tile_mask.shape[0]
    protos = unit_rows(lax.dynamic_slice_in_dim(prototypes, inner_pos * cols, cols, 0))
    both = jnp.concatenate([unit_rows(view_a), unit_rows(view_b)], axis=1)
    both = lax.all_gather(both, PART, axis=0, tiled=True)
    rows_a, rows_b = (both[:, :width], both[:, width:])
    hits = rows_a.shape[0]
    own_tile = (blk_pos * n_dp * n_sub + inner_pos) * tiles
    my_mask = lax.dynamic_slice_in_dim(tile_mask, own_tile, tiles, 1).astype(jnp.float32)
    onehot = (tile_region[:, None] == jnp.arange(regions, dtype=jnp.int32)[None, :]).astype(
        jnp.float32
    )
    flags = jnp.dot(onehot, my_mask) > 0.5
    active = jnp.broadcast_to(
        flags[:, None, :, None], (hits // hit_dev, hit_dev, tiles, TILE)
    ).reshape(hits, cols)

    def scores(rows):
        return jnp.einsum("rd,kd->rk", rows, protos, preferred_element_type=jnp.float32)

    code_exp = jnp.where(active, jnp.exp((scores(rows_a) - 1.0) / EPSILON), 0.0).astype(
        jnp.bfloat16
    )
    pred = jnp.where(active, jnp.exp((scores(rows_b) - 1.0) / SOFTMAX_TEMPER), 0.0)
    norm = jnp.sum(pred, axis=1)
    code = code_exp.astype(jnp.float32)
    row = jnp.ones((hits,), jnp.float32)
    for sweep in range(ITERS):
        col = 1.0 / jnp.sum(code * row[:, None], axis=0)
        part = jnp.sum(code * col[None, :], axis=1)
        if sweep == 0:
            part, norm = lax.psum((part, norm), PART)
        else:
            part = lax.psum(part, PART)
        row = 1.0 / part
    grad = ((pred / norm[:, None] - row[:, None] * code * col[None, :]) / SOFTMAX_TEMPER).astype(
        jnp.bfloat16
    )
    hit_part = jnp.dot(grad, protos, preferred_element_type=jnp.float32)
    grad_protos = jnp.einsum("rk,rd->kd", grad, rows_b, preferred_element_type=jnp.float32)
    return (lax.psum_scatter(hit_part, PART, scatter_dimension=0, tiled=True), grad_protos)


def solution(mesh):
    spread = P(("groups", "blk", "dp", "sub"), None)
    return jax.shard_map(
        body,
        mesh=mesh,
        in_specs=(spread, spread, P("blk", None), P(), P("groups")),
        out_specs=(spread, spread),
        check_vma=False,
    )
```

profile of v0, /device:TPU:0, one launch (start us, length us, event | category | flops | bytes accessed | tf_op | source)
XLA Modules:
  0.0 244.8 jit_solution(6231227928295905269)
XLA Ops:
  7.2 0.0 all-gather.2.cloned.1.call-start
  7.2 0.9 fusion.17
  8.1 0.9 fusion.19
  9.0 0.9 fusion.18
  9.9 0.6 pad_maximum_fusion
  10.5 0.0 all-gather.2.cloned.1.call-update
  10.5 0.0 reduce-scatter.2.cloned.1.call-start
  10.6 1.6 fusion.10
  12.2 0.9 convolution_compare_fusion
  13.1 38.3 %all-gather.2.cloned.1.call-done = bf16[1024,512]{1,0:T(8,128)(2,1)} async-done(((bf16[64,512]{1,0:T(8,128)(2,1)}), bf16[1024,512]{1,0:T(8,128)(2,1)}) %all-gather.2.cloned.1.call-update) | async-done | bytes 1048592 | tf_op jit(solution)/shard_map/all_gather | solution.py:31
  51.4 0.6 broadcast_in_dim.6
  52.0 4.3 %convert_reduce_fusion = (f32[2048]{0:T(1024)S(1)}, bf16[1024,2048]{1,0:T(8,128)(2,1)S(1)}) fusion(f32[2048]{0:T(1024)S(1)} %add_rsqrt_fusion, bf16[8192,256]{1,0:T(8,128)(2,1)} %param.7, s32[]{:T(128)S(6)} %select_n.14, bf16[1024,512]{1,0:T(8,128)(2,1)} %all-gather.2.cloned.1.call-done, pred[128,8,16,128]{3,2,1,0:T(8,128)(4,1)S(1)} %bitcast.11), kind=kOutput, calls=%fused_computation.6 | convolution fusion | flops 1087895552 | bytes 7880708 | tf_op jit(solution)/shard_map/rd,kd->rk/dot_general | solution.py:45
  56.3 0.0 copy-start
  56.4 2.0 copy-done
  58.3 0.9 fusion
  59.2 31.6 %psum.29 = f32[1024]{0:T(1024)S(1)} all-reduce(f32[1024]{0:T(1024)S(1)} %fusion), channel_id=1, replica_groups=mesh['groups'=2,'blk'=4,'dp'=2,'sub'=2] {'blk','dp','sub'}, use_global_device_ids=true, to_apply=%region_7.8 | all-reduce | flops 1024 | bytes 8192 | tf_op jit(solution)/shard_map/psum | solution.py:58
  90.8 0.0 copy-start.2
  90.8 3.2 %fusion.1 = f32[2048]{0:T(1024)S(1)} fusion(bf16[1024,2048]{1,0:T(8,128)(2,1)} %copy-done, f32[1024]{0:T(1024)S(1)} %broadcast_divide_fusion.5), kind=kLoop, calls=%fused_computation.8 | loop fusion | flops 6289408 | bytes 4206592 | tf_op jit(solution)/shard_map/reduce_sum | solution.py:55
  94.0 3.1 %fusion.2 = f32[1024]{0:T(1024)S(1)} fusion(bf16[1024,2048]{1,0:T(8,128)(2,1)} %copy-done, f32[2048]{0:T(1024)S(1)} %broadcast_divide_fusion.1), kind=kLoop, calls=%fused_computation.9 | loop fusion | flops 6290432 | bytes 4206592 | tf_op jit(solution)/shard_map/reduce_sum | solution.py:56
  97.1 29.7 %psum.30 = f32[1024]{0:T(1024)S(1)} all-reduce(f32[1024]{0:T(1024)S(1)} %fusion.2), channel_id=1, replica_groups=mesh['groups'=2,'blk'=4,'dp'=2,'sub'=2] {'blk','dp','sub'}, use_global_device_ids=true, to_apply=%region_10.11 | all-reduce | flops 1024 | bytes 8192 | tf_op jit(solution)/shard_map/psum | solution.py:60
  126.8 3.1 %fusion.3 = f32[2048]{0:T(1024)S(1)} fusion(bf16[1024,2048]{1,0:T(8,128)(2,1)} %copy-done, f32[1024]{0:T(1024)S(1)} %broadcast_divide_fusion.4), kind=kLoop, calls=%fused_computation.10 | loop fusion | flops 6289408 | bytes 4206592 | tf_op jit(solution)/shard_map/reduce_sum | solution.py:55
  129.9 3.1 %fusion.4 = f32[1024]{0:T(1024)S(1)} fusion(bf16[1024,2048]{1,0:T(8,128)(2,1)} %copy-done, f32[2048]{0:T(1024)S(1)} %broadcast_divide_fusion), kind=kLoop, calls=%fused_computation.11 | loop fusion | flops 6290432 | bytes 4206592 | tf_op jit(solution)/shard_map/reduce_sum | solution.py:56
  132.9 0.0 copy-done.2
  132.9 7.3 %fusion.9 = (f32[1024]{0:T(1024)S(1)}, f32[1024,2048]{1,0:T(8,128)}) fusion(pred[128,8,16,128]{3,2,1,0:T(8,128)(4,1)S(1)} %bitcast.12, f32[2048]{0:T(1024)S(1)} %add_rsqrt_fusion, bf16[8192,256]{1,0:T(8,128)(2,1)} %param.7, s32[]{:T(128)S(6)} %select_n.14, bf16[1024,512]{1,0:T(8,128)(2,1)S(1)} %copy-done.2), kind=kOutput, calls=%fused_computation.18 | convolution fusion | flops 1083702272 | bytes 12070916 | tf_op jit(solution)/shard_map/rd,kd->rk/dot_general | solution.py:45
  140.2 30.0 %all-reduce = (f32[1024]{0:T(1024)S(1)}, f32[1024]{0:T(1024)S(1)}) all-reduce(f32[1024]{0:T(1024)S(1)} %fusion.4, f32[1024]{0:T(1024)S(1)} %get-tuple-element.6), channel_id=1, replica_groups=mesh['groups'=2,'blk'=4,'dp'=2,'sub'=2] {'blk','dp','sub'}, use_global_device_ids=true, to_apply=%region_13.14 | all-reduce | flops 2048 | bytes 16384 | tf_op jit(solution)/shard_map/psum | solution.py:60
  170.2 7.4 %fusion.8 = bf16[1024,2048]{1,0:T(8,128)(2,1)S(1)} fusion(bf16[1024,2048]{1,0:T(8,128)(2,1)} %copy-done, f32[1024,2048]{1,0:T(8,128)} %get-tuple-element.7, pred[128,8,16,128]{3,2,1,0:T(8,128)(4,1)S(1)} %bitcast.13, f32[1024]{0:T(1024)S(1)} %broadcast_divide_fusion.3, f32[2048]{0:T(1024)S(1)} %broadcast_divide_fusion, f32[1024]{0:T(1024)S(1)} %get-tuple-element.3), kind=kLoop, calls=%fused_computation.15 | loop fusion | flops 20971520 | bytes 18890752 | tf_op jit(solution)/shard_map/convert_element_type | solution.py:62
  177.6 0.0 copy-start.1
  177.7 1.9 copy-done.1
  179.6 3.6 %fusion.25 = f32[1024,256]{1,0:T(8,128)} fusion(bf16[1024,2048]{1,0:T(8,128)(2,1)S(1)} %fusion.8, f32[2048]{0:T(1024)S(1)} %add_rsqrt_fusion, bf16[8192,256]{1,0:T(8,128)(2,1)} %param.7, s32[]{:T(128)S(6)} %select_n.14), kind=kOutput, calls=%fused_computation.52 | convolution fusion | flops 1075314688 | bytes 6299652 | tf_op jit(solution)/shard_map/dot_general | solution.py:65
  183.1 0.0 reduce-scatter.2.cloned.1.call-update
  183.2 4.8 %fusion.13 = f32[2048,256]{1,0:T(8,128)} fusion(bf16[1024,2048]{1,0:T(8,128)(2,1)} %copy-done.1, bf16[1024,512]{1,0:T(8,128)(2,1)S(1)} %copy-done.2), kind=kOutput, calls=%fused_computation.25 | convolution fusion | flops 1073741824 | bytes 6815744 | tf_op jit(solution)/shard_map/rk,rd->kd/dot_general | solution.py:66
  188.0 49.9 %reduce-scatter.2.cloned.1.call-done = f32[64,256]{1,0:T(8,128)} async-done(((f32[1024,256]{1,0:T(8,128)}), f32[64,256]{1,0:T(8,128)}) %reduce-scatter.2.cloned.1.call-update) | async-done | bytes 65552 | tf_op jit(solution)/shard_map/reduce_scatter | solution.py:67
  (9 shorter events, 0.0 us)
Async XLA Ops:
  7.2 44.2 %all-gather.2.cloned.1.call-start = ((), (), s32[]{:S(2)}) async-start(), calls=%async_computation.1 | async-start | bytes 1114112 | tf_op jit(solution)/shard_map/all_gather | solution.py:31
  10.5 227.4 %reduce-scatter.2.cloned.1.call-start = ((), (), s32[]{:S(2)}) async-start(), calls=%async_computation.2 | async-start | bytes 1114112 | tf_op jit(solution)/shard_map/reduce_scatter | solution.py:67
  56.3 2.0 copy-start
  90.8 42.1 %copy-start.2 = (bf16[1024,512]{1,0:T(8,128)(2,1)S(1)}, bf16[1024,512]{1,0:T(8,128)(2,1)}, u32[]{:S(2)}) copy-start(bf16[1024,512]{1,0:T(8,128)(2,1)} %all-gather.2.cloned.1.call-done) | copy-start | bytes 3145732
  177.6 1.9 copy-start.1
Sparse Core Ops, SparseCore 0:
  10.7 40.6 all-gather.1
  183.3 54.6 reduce-scatter.1
where the time goes:
time: 245 us
  blocking collectives  91.2 us (37%)
  waiting for transfers between devices  88.3 us (36%)
  other arithmetic  25.6 us (10%)
  matrix products  20.9 us (9%)
  between operations  14.2 us (6%)
  local copies, waits for them, and re-layouts  4.48 us (2%)
    psum x2, blocking collectives, body(): part = lax.psum(part, PART)  59.6 us
    reduce_scatter x1, waiting for transfers between devices, body(): lax.psum_scatter(hit_part, PART, scatter_dimension=0, tiled=True)  49.9 us
    all_gather x1, waiting for transfers between devices, body(): both = lax.all_gather(both, PART, axis=0, tiled=True)  38.3 us
    psum x1, blocking collectives, body(): part, norm = lax.psum((part, norm), PART)  31.6 us
    dot_general x2, matrix products, scores(): jnp.einsum('rd,kd->rk', rows, protos, preferred_element_type=jnp.float32)  11.6 us
    convert_element_type x1, other arithmetic, body(): ((pred / norm[:, None] - row[:, None] * code * col[None, :]) / SOFTMAX_TE...  7.44 us
    reduce_sum x3, other arithmetic, body(): part = jnp.sum(code * col[None, :], axis=1)  7.06 us
    reduce_sum x2, other arithmetic, body(): col = 1.0 / jnp.sum(code * row[:, None], axis=0)  6.24 us
  transfers between devices with their start and end apart: 2, of which 2 were waited for; matrix products, arithmetic and copies ran while one was open for 3% of the time, Pallas kernels for 0%

commit v1 on v0

--- a/solution.py
+++ b/solution.py
@@ -8,6 +8,10 @@
 SOFTMAX_TEMPER = 0.1
 EPSILON = 0.05
 PART = ("blk", "dp", "sub")
+
+
+def fill_samples_on(group_axis, message, dev_axis):
+    return jax.lax.psum(jax.lax.psum(message, dev_axis), axis_name=group_axis)
 
 
 def unit_rows(matrix):
@@ -55,7 +59,7 @@
         col = 1.0 / jnp.sum(code * row[:, None], axis=0)
         part = jnp.sum(code * col[None, :], axis=1)
         if sweep == 0:
-            part, norm = lax.psum((part, norm), PART)
+            part, norm = fill_samples_on("blk", (part, norm), dev_axis=("dp", "sub"))
         else:
             part = lax.psum(part, PART)
         row = 1.0 / part

time: 245 us -> 229 us (0.935)
  blocking collectives: 91.2 us -> 76.1 us
    psum x1 -> x2, blocking collectives: 31.6 us -> 16.9 us  [fill_samples_on(): return jax.lax.psum(jax.lax.psum(message, dev_axis), axis_name=group_axis)]
where the time goes in v1:
time: 229 us; the launch traced here: 228 us
  waiting for transfers between devices  88.3 us (39%)
  blocking collectives  76.1 us (33%)
  other arithmetic  25.5 us (11%)
  matrix products  21.5 us (9%)
  between operations  14.2 us (6%)
  local copies, waits for them, and re-layouts  2.53 us (1%)
    psum x2, blocking collectives, body(): part = lax.psum(part, PART)  59.2 us
    reduce_scatter x1, waiting for transfers between devices, body(): lax.psum_scatter(hit_part, PART, scatter_dimension=0, tiled=True)  49.9 us
    all_gather x1, waiting for transfers between devices, body(): both = lax.all_gather(both, PART, axis=0, tiled=True)  38.3 us
    psum x2, blocking collectives, fill_samples_on(): return jax.lax.psum(jax.lax.psum(message, dev_axis), axis_name=group_axis)  16.9 us
    dot_general x2, matrix products, scores(): jnp.einsum('rd,kd->rk', rows, protos, preferred_element_type=jnp.float32)  12.2 us
    convert_element_type x1, other arithmetic, body(): ((pred / norm[:, None] - row[:, None] * code * col[None, :]) / SOFTMAX_TE...  7.43 us
    reduce_sum x3, other arithmetic, body(): part = jnp.sum(code * col[None, :], axis=1)  7.06 us
    reduce_sum x2, other arithmetic, body(): col = 1.0 / jnp.sum(code * row[:, None], axis=0)  6.15 us
  transfers between devices with their start and end apart: 2, of which 2 were waited for; matrix products, arithmetic and copies ran while one was open for 3% of the time, Pallas kernels for 0%

profile of v1, /device:TPU:0, one launch (start us, length us, event | category | flops | bytes accessed | tf_op | source)
XLA Modules:
  0.0 228.2 jit_solution(5296620620910135981)
XLA Ops:
  7.2 0.0 all-gather.2.cloned.1.call-start
  7.2 0.9 fusion.17
  8.1 0.9 fusion.19
  9.0 0.9 fusion.18
  9.9 0.6 pad_maximum_fusion
  10.5 0.0 all-gather.2.cloned.1.call-update
  10.5 0.0 reduce-scatter.2.cloned.1.call-start
  10.6 1.6 fusion.10
  12.2 0.9 convolution_compare_fusion
  13.1 38.3 %all-gather.2.cloned.1.call-done = bf16[1024,512]{1,0:T(8,128)(2,1)} async-done(((bf16[64,512]{1,0:T(8,128)(2,1)}), bf16[1024,512]{1,0:T(8,128)(2,1)}) %all-gather.2.cloned.1.call-update) | async-done | bytes 1048592 | tf_op jit(solution)/shard_map/all_gather | solution.py:35
  51.4 0.6 broadcast_in_dim.6
  52.0 0.0 copy-start.2
  52.0 4.4 %convert_reduce_fusion = (f32[2048]{0:T(1024)S(1)}, bf16[1024,2048]{1,0:T(8,128)(2,1)S(1)}) fusion(f32[2048]{0:T(1024)S(1)} %add_rsqrt_fusion, bf16[8192,256]{1,0:T(8,128)(2,1)} %param.7, s32[]{:T(128)S(6)} %select_n.14, bf16[1024,512]{1,0:T(8,128)(2,1)} %all-gather.2.cloned.1.call-done, pred[128,8,16,128]{3,2,1,0:T(8,128)(4,1)S(1)} %bitcast.11), kind=kOutput, calls=%fused_computation.6 | convolution fusion | flops 1087895552 | bytes 7880708 | tf_op jit(solution)/shard_map/rd,kd->rk/dot_general | solution.py:49
  56.4 0.0 copy-start
  56.5 0.9 fusion
  57.4 0.0 copy-done.2
  57.4 7.8 %fusion.9 = (f32[1024]{0:T(1024)S(1)}, f32[1024,2048]{1,0:T(8,128)}) fusion(pred[128,8,16,128]{3,2,1,0:T(8,128)(4,1)S(1)} %bitcast.12, f32[2048]{0:T(1024)S(1)} %add_rsqrt_fusion, bf16[8192,256]{1,0:T(8,128)(2,1)} %param.7, s32[]{:T(128)S(6)} %select_n.14, bf16[1024,512]{1,0:T(8,128)(2,1)S(1)} %copy-done.2), kind=kOutput, calls=%fused_computation.18 | convolution fusion | flops 1083702272 | bytes 12070916 | tf_op jit(solution)/shard_map/rd,kd->rk/dot_general | solution.py:49
  65.2 0.0 copy-done
  65.2 6.1 %all-reduce = (f32[1024]{0:T(1024)S(1)}, f32[1024]{0:T(1024)S(1)}) all-reduce(f32[1024]{0:T(1024)S(1)} %fusion, f32[1024]{0:T(1024)S(1)} %get-tuple-element.8), channel_id=1, replica_groups=mesh['groups'=2,'blk'=4,'dp'=2,'sub'=2] {'dp','sub'}, use_global_device_ids=true, to_apply=%region_8.9 | all-reduce | flops 2048 | bytes 16384 | tf_op jit(solution)/shard_map/psum | solution.py:14
  71.3 10.8 %all-reduce.1 = (f32[1024]{0:T(1024)S(1)}, f32[1024]{0:T(1024)S(1)}) all-reduce(f32[1024]{0:T(1024)S(1)} %get-tuple-element.2, f32[1024]{0:T(1024)S(1)} %get-tuple-element.3), channel_id=1, replica_groups=mesh['groups'=2,'blk'=4,'dp'=2,'sub'=2] {'blk'}, use_global_device_ids=true, to_apply=%region_9.10 | all-reduce | flops 2048 | bytes 16384 | tf_op jit(solution)/shard_map/psum | solution.py:14
  82.1 3.1 %fusion.1 = f32[2048]{0:T(1024)S(1)} fusion(bf16[1024,2048]{1,0:T(8,128)(2,1)} %copy-done, f32[1024]{0:T(1024)S(1)} %broadcast_divide_fusion.5), kind=kLoop, calls=%fused_computation.8 | loop fusion | flops 6289408 | bytes 4206592 | tf_op jit(solution)/shard_map/reduce_sum | solution.py:59
  85.2 3.1 %fusion.2 = f32[1024]{0:T(1024)S(1)} fusion(bf16[1024,2048]{1,0:T(8,128)(2,1)} %copy-done, f32[2048]{0:T(1024)S(1)} %broadcast_divide_fusion.1), kind=kLoop, calls=%fused_computation.9 | loop fusion | flops 6290432 | bytes 4206592 | tf_op jit(solution)/shard_map/reduce_sum | solution.py:60
  88.3 29.7 %psum.46 = f32[1024]{0:T(1024)S(1)} all-reduce(f32[1024]{0:T(1024)S(1)} %fusion.2), channel_id=1, replica_groups=mesh['groups'=2,'blk'=4,'dp'=2,'sub'=2] {'blk','dp','sub'}, use_global_device_ids=true, to_apply=%region_12.13 | all-reduce | flops 1024 | bytes 8192 | tf_op jit(solution)/shard_map/psum | solution.py:64
  118.0 3.1 %fusion.3 = f32[2048]{0:T(1024)S(1)} fusion(bf16[1024,2048]{1,0:T(8,128)(2,1)} %copy-done, f32[1024]{0:T(1024)S(1)} %broadcast_divide_fusion.4), kind=kLoop, calls=%fused_computation.10 | loop fusion | flops 6289408 | bytes 4206592 | tf_op jit(solution)/shard_map/reduce_sum | solution.py:59
  121.1 3.1 %fusion.4 = f32[1024]{0:T(1024)S(1)} fusion(bf16[1024,2048]{1,0:T(8,128)(2,1)} %copy-done, f32[2048]{0:T(1024)S(1)} %broadcast_divide_fusion), kind=kLoop, calls=%fused_computation.11 | loop fusion | flops 6290432 | bytes 4206592 | tf_op jit(solution)/shard_map/reduce_sum | solution.py:60
  124.1 29.5 %psum.47 = f32[1024]{0:T(1024)S(1)} all-reduce(f32[1024]{0:T(1024)S(1)} %fusion.4), channel_id=1, replica_groups=mesh['groups'=2,'blk'=4,'dp'=2,'sub'=2] {'blk','dp','sub'}, use_global_device_ids=true, to_apply=%region_15.16 | all-reduce | flops 1024 | bytes 8192 | tf_op jit(solution)/shard_map/psum | solution.py:64
  153.6 7.4 %fusion.8 = bf16[1024,2048]{1,0:T(8,128)(2,1)S(1)} fusion(bf16[1024,2048]{1,0:T(8,128)(2,1)} %copy-done, f32[1024,2048]{1,0:T(8,128)} %get-tuple-element.9, pred[128,8,16,128]{3,2,1,0:T(8,128)(4,1)S(1)} %bitcast.13, f32[1024]{0:T(1024)S(1)} %broadcast_divide_fusion.3, f32[2048]{0:T(1024)S(1)} %broadcast_divide_fusion, f32[1024]{0:T(1024)S(1)} %get-tuple-element.5), kind=kLoop, calls=%fused_computation.15 | loop fusion | flops 20971520 | bytes 18890752 | tf_op jit(solution)/shard_map/convert_element_type | solution.py:66
  161.1 0.0 copy-start.1
  161.1 1.9 copy-done.1
  163.0 3.6 %fusion.25 = f32[1024,256]{1,0:T(8,128)} fusion(bf16[1024,2048]{1,0:T(8,128)(2,1)S(1)} %fusion.8, f32[2048]{0:T(1024)S(1)} %add_rsqrt_fusion, bf16[8192,256]{1,0:T(8,128)(2,1)} %param.7, s32[]{:T(128)S(6)} %select_n.14), kind=kOutput, calls=%fused_computation.52 | convolution fusion | flops 1075314688 | bytes 6299652 | tf_op jit(solution)/shard_map/dot_general | solution.py:69
  166.6 0.0 reduce-scatter.2.cloned.1.call-update
  166.6 4.9 %fusion.13 = f32[2048,256]{1,0:T(8,128)} fusion(bf16[1024,2048]{1,0:T(8,128)(2,1)} %copy-done.1, bf16[1024,512]{1,0:T(8,128)(2,1)S(1)} %copy-done.2), kind=kOutput, calls=%fused_computation.25 | convolution fusion | flops 1073741824 | bytes 6815744 | tf_op jit(solution)/shard_map/rk,rd->kd/dot_general | solution.py:70
  171.5 49.9 %reduce-scatter.2.cloned.1.call-done = f32[64,256]{1,0:T(8,128)} async-done(((f32[1024,256]{1,0:T(8,128)}), f32[64,256]{1,0:T(8,128)}) %reduce-scatter.2.cloned.1.call-update) | async-done | bytes 65552 | tf_op jit(solution)/shard_map/reduce_scatter | solution.py:71
  (9 shorter events, 0.0 us)
Async XLA Ops:
  7.2 44.2 %all-gather.2.cloned.1.call-start = ((), (), s32[]{:S(2)}) async-start(), calls=%async_computation.1 | async-start | bytes 1114112 | tf_op jit(solution)/shard_map/all_gather | solution.py:35
  10.5 210.9 %reduce-scatter.2.cloned.1.call-start = ((), (), s32[]{:S(2)}) async-start(), calls=%async_computation.2 | async-start | bytes 1114112 | tf_op jit(solution)/shard_map/reduce_scatter | solution.py:71
  52.0 5.3 %copy-start.2 = (bf16[1024,512]{1,0:T(8,128)(2,1)S(1)}, bf16[1024,512]{1,0:T(8,128)(2,1)}, u32[]{:S(2)}) copy-start(bf16[1024,512]{1,0:T(8,128)(2,1)} %all-gather.2.cloned.1.call-done) | copy-start | bytes 3145732
  56.4 8.7 %copy-start = (bf16[1024,2048]{1,0:T(8,128)(2,1)}, bf16[1024,2048]{1,0:T(8,128)(2,1)S(1)}, u32[]{:S(2)}) copy-start(bf16[1024,2048]{1,0:T(8,128)(2,1)S(1)} %get-tuple-element.7) | copy-start | bytes 12582916
  161.1 1.9 copy-start.1
Sparse Core Ops, SparseCore 0:
  10.7 40.6 all-gather.1
  166.7 54.6 reduce-scatter.1
